TPU v7x, 256 devices: a whole 4x4x8 slice. The times are simulated.
256 devices in a mesh: expert: 2 (over z_lo), batch: 4 (over x), seq: 32 (over y, z_hi, core).
Axes of the slice: x: 4, y: 4, z: 8 (z_hi: 4, z_lo: 2; z = z_hi * 2 + z_lo), core: 2. Of those that a mesh axis runs over, the one named last changes fastest.
Arguments:
- queries: bfloat16 [2, 4, 2, 3072, 4096], P('expert', 'batch', None, 'seq'), may hold values from -36 to 36
- keys: bfloat16 [2, 4, 2, 3072, 4096], P('expert', 'batch', None, 'seq'), may hold values from -21 to 21
- values: bfloat16 [2, 4, 2, 3072, 4096], P('expert', 'batch', None, 'seq'), may hold values from -6 to 6
- latents: bfloat16 [2, 4, 3072, 4096], P('expert', 'batch', 'seq'), may hold values from -6 to 6
- gain: bfloat16 [2, 4096], P('expert'), may hold values from 0.099609375 to 1.8984375
- steps_table: int32 [2, 4], P('expert', 'batch'), may hold values from 0 to 38
- flags: int32 [4], P('batch'), may hold values 0 or 1
Outputs:
- denoised: bfloat16 [2, 4, 3072, 4096], P('expert', 'batch', 'seq')
- next_latents: bfloat16 [2, 4, 3072, 4096], P('expert', 'batch', 'seq')
All inputs are finite; a program needn't handle non-finite values. No bound on the sum of `flags` on one device may be relied on, other than what follows from the above.
Results may differ from a plain program's by a relative error of at most 0.006.
Values may be sent and summed in bfloat16 or wider, within the bound.
No kernel may reach another device: no remote copies, remote signals or barrier semaphores. Data moves between devices by JAX's collectives and lax.ppermute only.
A program may use at most 64 MiB of HBM per device.

v0:
```python
import jax
import jax.numpy as jnp
from jax import lax
from jax.sharding import Mesh
from jax.sharding import PartitionSpec as P

HDIM = 128
STEPS = 40
SEQ = ("seq_0", "seq_1", "seq_2")
GUIDANCE = 3.5
flow_shift = 5.0


def split_up(value, dim, peers):
    lengths = value.shape
    tiles = value.reshape(*lengths[:dim], peers, lengths[dim] // peers, *lengths[dim + 1 :])
    return jnp.moveaxis(tiles, dim, 0)


def joined_along(tiles, dim):
    tiles = jnp.moveaxis(tiles, 0, dim)
    lengths = tiles.shape
    return tiles.reshape(*lengths[:dim], lengths[dim] * lengths[dim + 1], *lengths[dim + 2 :])


def exchange_in_order(tiles, axes, sequence):
    inside = tiles.shape[1:]
    out = tiles.reshape(*(lax.axis_size(a) for a in axes), *inside)
    for k in sequence:
        out = lax.all_to_all(out, axes[k], k, k, tiled=True)
    return out.reshape(-1, *inside)


def exchange_by_chip(value, groups, sequence, split_dim, concat_dim):
    peers = lax.axis_size(groups[0]) * lax.axis_size(groups[1])
    tiles = split_up(value, split_dim, peers)
    return joined_along(exchange_in_order(tiles, groups, sequence), concat_dim)


def from_partner(block, axis, bit):
    count = lax.axis_size(axis)
    route = []
    for low in range(count):
        high = low | 1 << bit
        if high != low and high < count:
            route += [(low, high), (high, low)]
    return lax.ppermute(block, axis, route)


def sigma_of(step):
    level = 1.0 - step.astype(jnp.float32) / STEPS
    return flow_shift * level / (1.0 + (flow_shift - 1.0) * level)


def combine(cond, uncond):
    base = uncond.astype(jnp.float32)
    return (base + GUIDANCE * (cond.astype(jnp.float32) - base)).astype(jnp.bfloat16)


def attend(stacked):
    query_heads, key_heads, value_heads = stacked
    items, length, width_dev = query_heads.shape
    heads_dev = width_dev // HDIM
    block = 512
    key_rows = key_heads.reshape(items, length, heads_dev, HDIM)
    value_rows = value_heads.reshape(items, length, heads_dev, HDIM)
    query_blocks = query_heads.reshape(items, length // block, block, heads_dev, HDIM).transpose(
        1, 0, 2, 3, 4
    )

    def one_block(query_part):
        scores = jnp.einsum(
            "nqhd,nkhd->nhqk", query_part, key_rows, preferred_element_type=jnp.float32
        ) * HDIM ** (-0.5)
        weights = jax.nn.softmax(scores, axis=-1).astype(jnp.bfloat16)
        return jnp.einsum(
            "nhqk,nkhd->nqhd", weights, value_rows, preferred_element_type=jnp.float32
        ).astype(jnp.bfloat16)

    result = lax.map(one_block, query_blocks)
    return result.transpose(1, 0, 2, 3, 4).reshape(items, length, width_dev)


def per_device(queries, keys, values, latents, gain, steps_table, flags):
    attended = attend(
        (
            exchange_by_chip(queries[0, 0], (("seq_0", "seq_1"), "seq_2"), (0, 1), 2, 1),
            exchange_by_chip(keys[0, 0], (("seq_0", "seq_1"), "seq_2"), (0, 1), 2, 1),
            exchange_by_chip(values[0, 0], (("seq_0", "seq_1"), "seq_2"), (0, 1), 2, 1),
        )
    )
    guided = lax.all_to_all(
        combine(attended[0], attended[1]), SEQ, split_axis=0, concat_axis=1, tiled=True
    )
    guided_f32 = guided.astype(jnp.float32)
    scale = lax.rsqrt(jnp.mean(guided_f32 * guided_f32, axis=-1, keepdims=True) + 1e-06)
    velocity = guided_f32 * scale * gain[0].astype(jnp.float32)[None, :]
    step_now = steps_table[0, 0]
    sigma_now = sigma_of(step_now)
    sigma_next = sigma_of(step_now + 1)
    current = latents[0, 0].astype(jnp.float32)
    denoised = (current - sigma_now * velocity).astype(jnp.bfloat16)
    moved = (current + (sigma_next - sigma_now) * velocity).astype(jnp.bfloat16)
    partner = from_partner(moved, "expert", 0)
    next_latents = jnp.where(flags[0] == 1, partner, moved)
    return (denoised[None, None], next_latents[None, None])


def solution(mesh):
    torus = Mesh(
        mesh.devices.reshape(mesh.shape["expert"], mesh.shape["batch"], 4, 4, 2),
        ("expert", "batch", "seq_0", "seq_1", "seq_2"),
    )
    placed = (
        P("expert", "batch", None, SEQ, None),
        P("expert", "batch", None, SEQ, None),
        P("expert", "batch", None, SEQ, None),
        P("expert", "batch", SEQ, None),
        P("expert", None),
        P("expert", "batch"),
        P("batch"),
    )
    return jax.shard_map(
        per_device,
        mesh=torus,
        in_specs=placed,
        out_specs=(P("expert", "batch", SEQ, None), P("expert", "batch", SEQ, None)),
        check_vma=False,
    )
```

profile of v0, /device:TPU:6, one launch (start us, length us, event | category | flops | bytes accessed | tf_op | source)
XLA Modules:
  0.0 393.9 jit_solution(4078479257126038862)
XLA Ops:
  4.1 11.3 %all-to-all-start.2 = ((bf16[16,2,2,96,128]{4,3,1,2,0:T(8,128)(2,1)}), bf16[16,2,2,96,128]{4,3,1,2,0:T(8,128)(2,1)S(1)}, u32[]{:S(2)}, u32[]{:S(2)}) async-start(bf16[16,2,2,96,128]{4,3,1,2,0:T(8,128)(2,1)} %copy.43), calls=%async_computation.2 | async-start | bytes 3145728 | tf_op jit(solution)/shard_map/all_to_all | solution.py:30
  17.6 39.5 %all-to-all-done.2 = bf16[16,2,2,96,128]{4,3,1,2,0:T(8,128)(2,1)S(1)} async-done(((bf16[16,2,2,96,128]{4,3,1,2,0:T(8,128)(2,1)}), bf16[16,2,2,96,128]{4,3,1,2,0:T(8,128)(2,1)S(1)}, u32[]{:S(2)}, u32[]{:S(2)}) %all-to-all-start.2) | async-done | bytes 1572896 | tf_op jit(solution)/shard_map/all_to_all | solution.py:30
  57.2 5.0 %all_to_all.40 = bf16[16,2,2,96,128]{4,3,0,2,1:T(8,128)(2,1)S(1)} all-to-all(bf16[16,2,2,96,128]{4,3,0,2,1:T(8,128)(2,1)S(1)} %copy.44), channel_id=1, replica_groups=mesh['expert'=2,'batch'=4,'seq_0'=4,'seq_1'=4,'seq_2'=2] {'seq_2'}, dimensions={1} | all-to-all | bytes 3145728 | tf_op jit(solution)/shard_map/all_to_all | solution.py:30
  62.2 3.7 all-to-all-start.4
  69.5 37.3 %all-to-all-done.4 = bf16[16,2,2,96,128]{4,3,1,2,0:T(8,128)(2,1)S(1)} async-done(((bf16[16,2,2,96,128]{4,3,1,2,0:T(8,128)(2,1)}), bf16[16,2,2,96,128]{4,3,1,2,0:T(8,128)(2,1)S(1)}, u32[]{:S(2)}, u32[]{:S(2)}) %all-to-all-start.4) | async-done | bytes 1572896 | tf_op jit(solution)/shard_map/all_to_all | solution.py:30
  106.8 5.2 %all-to-all-start = ((bf16[16,2,2,96,128]{4,3,1,2,0:T(8,128)(2,1)}), bf16[16,2,2,96,128]{4,3,1,2,0:T(8,128)(2,1)}, u32[]{:S(2)}, u32[]{:S(2)}) async-start(bf16[16,2,2,96,128]{4,3,1,2,0:T(8,128)(2,1)} %copy.39), calls=%async_computation | async-start | bytes 3145728 | tf_op jit(solution)/shard_map/all_to_all | solution.py:30
  113.6 36.0 %all-to-all-done = bf16[16,2,2,96,128]{4,3,1,2,0:T(8,128)(2,1)} async-done(((bf16[16,2,2,96,128]{4,3,1,2,0:T(8,128)(2,1)}), bf16[16,2,2,96,128]{4,3,1,2,0:T(8,128)(2,1)}, u32[]{:S(2)}, u32[]{:S(2)}) %all-to-all-start) | async-done | bytes 1572896 | tf_op jit(solution)/shard_map/all_to_all | solution.py:30
  149.6 3.7 all-to-all-start.5
  153.2 2.7 copy.40
  155.9 4.8 %all-to-all-start.1 = ((bf16[16,2,2,96,128]{4,3,0,2,1:T(8,128)(2,1)}), bf16[16,2,2,96,128]{4,3,0,2,1:T(8,128)(2,1)}, u32[]{:S(2)}, u32[]{:S(2)}) async-start(bf16[16,2,2,96,128]{4,3,0,2,1:T(8,128)(2,1)} %copy.40), calls=%async_computation.1 | async-start | bytes 3145728 | tf_op jit(solution)/shard_map/all_to_all | solution.py:30
  165.0 173.4 %while.10 = (s32[]{:T(128)}, bf16[6,2,512,1,128]{4,2,1,3,0:T(8,128)(2,1)}, bf16[6,2,512,1,128]{4,2,0,1,3:T(8,128)(2,1)S(1)}, bf16[2,3072,1,128]{3,1,0,2:T(8,128)...) while((s32[]{:T(128)}, bf16[6,2,512,1,128]{4,2,1,3,0:T(8,128)(2,1)}, ...), condition=%wide.region_3.4_spmd, body=%wide.region_0.3_spmd.sunk | while | flops 1639062528 | bytes 54009940 | solution.py:80
  165.0 6.3 %fusion.50 = f32[2,512,3072]{2,1,0:T(8,128)} fusion(bf16[2,3072,1,128]{3,1,0,2:T(8,128)(2,1)S(1)} %get-tuple-element.110, bf16[6,2,512,1,128]{4,2,0,1,3:T(8,128)(2,1)S(1)} %get-tuple-element.109, s32[]{:T(128)S(6)} %copy.70), kind=kOutput, calls=%fused_computation.8.clone.1 | convolution fusion | flops 805306368 | bytes 14417924 | tf_op jit(solution)/shard_map/while/body/eval_jaxpr/nqhd,nkhd->nhqk/dot_general | solution.py:72
  171.3 11.2 %fusion.51 = f32[2,512]{1,0:T(2,128)S(1)} fusion(f32[2,512,3072]{2,1,0:T(8,128)} %fusion.50), kind=kOutput, calls=%fused_computation.37.clone.1 | output fusion | flops 12585983 | bytes 12587008 | tf_op jit(solution)/shard_map/while/body/eval_jaxpr/sub | solution.py:75
  182.5 11.4 %fusion.52 = bf16[6,2,512,1,128]{4,2,1,3,0:T(8,128)(2,1)} fusion(bf16[6,2,512,1,128]{4,2,1,3,0:T(8,128)(2,1)} %get-tuple-element.102, s32[]{:T(128)S(6)} %copy.70, bf16[2,3072,1,128]{3,1,0,2:T(8,128)(2,1)} %get-tuple-element.111, f32[2,512]{1,0:T(2,128)S(1)} %fusion.51, f32[2,512,3072]{2,1,0:T(8,128)} %fusion.50), kind=kOutput, calls=%fused_computation.12.clone.1 | convolution fusion | flops 821170176 | bytes 27004932 | tf_op jit(solution)/shard_map/while/body/eval_jaxpr/nhqk,nkhd->nqhd/dot_general | solution.py:76
  193.9 6.3 %fusion.50 = f32[2,512,3072]{2,1,0:T(8,128)} fusion(bf16[2,3072,1,128]{3,1,0,2:T(8,128)(2,1)S(1)} %get-tuple-element.110, bf16[6,2,512,1,128]{4,2,0,1,3:T(8,128)(2,1)S(1)} %get-tuple-element.109, s32[]{:T(128)S(6)} %copy.70), kind=kOutput, calls=%fused_computation.8.clone.1 | convolution fusion | flops 805306368 | bytes 14417924 | tf_op jit(solution)/shard_map/while/body/eval_jaxpr/nqhd,nkhd->nhqk/dot_general | solution.py:72
  200.2 11.2 %fusion.51 = f32[2,512]{1,0:T(2,128)S(1)} fusion(f32[2,512,3072]{2,1,0:T(8,128)} %fusion.50), kind=kOutput, calls=%fused_computation.37.clone.1 | output fusion | flops 12585983 | bytes 12587008 | tf_op jit(solution)/shard_map/while/body/eval_jaxpr/sub | solution.py:75
  211.4 11.4 %fusion.52 = bf16[6,2,512,1,128]{4,2,1,3,0:T(8,128)(2,1)} fusion(bf16[6,2,512,1,128]{4,2,1,3,0:T(8,128)(2,1)} %get-tuple-element.102, s32[]{:T(128)S(6)} %copy.70, bf16[2,3072,1,128]{3,1,0,2:T(8,128)(2,1)} %get-tuple-element.111, f32[2,512]{1,0:T(2,128)S(1)} %fusion.51, f32[2,512,3072]{2,1,0:T(8,128)} %fusion.50), kind=kOutput, calls=%fused_computation.12.clone.1 | convolution fusion | flops 821170176 | bytes 27004932 | tf_op jit(solution)/shard_map/while/body/eval_jaxpr/nhqk,nkhd->nqhd/dot_general | solution.py:76
  222.8 6.3 %fusion.50 = f32[2,512,3072]{2,1,0:T(8,128)} fusion(bf16[2,3072,1,128]{3,1,0,2:T(8,128)(2,1)S(1)} %get-tuple-element.110, bf16[6,2,512,1,128]{4,2,0,1,3:T(8,128)(2,1)S(1)} %get-tuple-element.109, s32[]{:T(128)S(6)} %copy.70), kind=kOutput, calls=%fused_computation.8.clone.1 | convolution fusion | flops 805306368 | bytes 14417924 | tf_op jit(solution)/shard_map/while/body/eval_jaxpr/nqhd,nkhd->nhqk/dot_general | solution.py:72
  229.1 11.2 %fusion.51 = f32[2,512]{1,0:T(2,128)S(1)} fusion(f32[2,512,3072]{2,1,0:T(8,128)} %fusion.50), kind=kOutput, calls=%fused_computation.37.clone.1 | output fusion | flops 12585983 | bytes 12587008 | tf_op jit(solution)/shard_map/while/body/eval_jaxpr/sub | solution.py:75
  240.3 11.4 %fusion.52 = bf16[6,2,512,1,128]{4,2,1,3,0:T(8,128)(2,1)} fusion(bf16[6,2,512,1,128]{4,2,1,3,0:T(8,128)(2,1)} %get-tuple-element.102, s32[]{:T(128)S(6)} %copy.70, bf16[2,3072,1,128]{3,1,0,2:T(8,128)(2,1)} %get-tuple-element.111, f32[2,512]{1,0:T(2,128)S(1)} %fusion.51, f32[2,512,3072]{2,1,0:T(8,128)} %fusion.50), kind=kOutput, calls=%fused_computation.12.clone.1 | convolution fusion | flops 821170176 | bytes 27004932 | tf_op jit(solution)/shard_map/while/body/eval_jaxpr/nhqk,nkhd->nqhd/dot_general | solution.py:76
  251.7 6.3 %fusion.50 = f32[2,512,3072]{2,1,0:T(8,128)} fusion(bf16[2,3072,1,128]{3,1,0,2:T(8,128)(2,1)S(1)} %get-tuple-element.110, bf16[6,2,512,1,128]{4,2,0,1,3:T(8,128)(2,1)S(1)} %get-tuple-element.109, s32[]{:T(128)S(6)} %copy.70), kind=kOutput, calls=%fused_computation.8.clone.1 | convolution fusion | flops 805306368 | bytes 14417924 | tf_op jit(solution)/shard_map/while/body/eval_jaxpr/nqhd,nkhd->nhqk/dot_general | solution.py:72
  258.0 11.2 %fusion.51 = f32[2,512]{1,0:T(2,128)S(1)} fusion(f32[2,512,3072]{2,1,0:T(8,128)} %fusion.50), kind=kOutput, calls=%fused_computation.37.clone.1 | output fusion | flops 12585983 | bytes 12587008 | tf_op jit(solution)/shard_map/while/body/eval_jaxpr/sub | solution.py:75
  269.2 11.4 %fusion.52 = bf16[6,2,512,1,128]{4,2,1,3,0:T(8,128)(2,1)} fusion(bf16[6,2,512,1,128]{4,2,1,3,0:T(8,128)(2,1)} %get-tuple-element.102, s32[]{:T(128)S(6)} %copy.70, bf16[2,3072,1,128]{3,1,0,2:T(8,128)(2,1)} %get-tuple-element.111, f32[2,512]{1,0:T(2,128)S(1)} %fusion.51, f32[2,512,3072]{2,1,0:T(8,128)} %fusion.50), kind=kOutput, calls=%fused_computation.12.clone.1 | convolution fusion | flops 821170176 | bytes 27004932 | tf_op jit(solution)/shard_map/while/body/eval_jaxpr/nhqk,nkhd->nqhd/dot_general | solution.py:76
  280.6 6.3 %fusion.50 = f32[2,512,3072]{2,1,0:T(8,128)} fusion(bf16[2,3072,1,128]{3,1,0,2:T(8,128)(2,1)S(1)} %get-tuple-element.110, bf16[6,2,512,1,128]{4,2,0,1,3:T(8,128)(2,1)S(1)} %get-tuple-element.109, s32[]{:T(128)S(6)} %copy.70), kind=kOutput, calls=%fused_computation.8.clone.1 | convolution fusion | flops 805306368 | bytes 14417924 | tf_op jit(solution)/shard_map/while/body/eval_jaxpr/nqhd,nkhd->nhqk/dot_general | solution.py:72
  286.9 11.2 %fusion.51 = f32[2,512]{1,0:T(2,128)S(1)} fusion(f32[2,512,3072]{2,1,0:T(8,128)} %fusion.50), kind=kOutput, calls=%fused_computation.37.clone.1 | output fusion | flops 12585983 | bytes 12587008 | tf_op jit(solution)/shard_map/while/body/eval_jaxpr/sub | solution.py:75
  298.1 11.4 %fusion.52 = bf16[6,2,512,1,128]{4,2,1,3,0:T(8,128)(2,1)} fusion(bf16[6,2,512,1,128]{4,2,1,3,0:T(8,128)(2,1)} %get-tuple-element.102, s32[]{:T(128)S(6)} %copy.70, bf16[2,3072,1,128]{3,1,0,2:T(8,128)(2,1)} %get-tuple-element.111, f32[2,512]{1,0:T(2,128)S(1)} %fusion.51, f32[2,512,3072]{2,1,0:T(8,128)} %fusion.50), kind=kOutput, calls=%fused_computation.12.clone.1 | convolution fusion | flops 821170176 | bytes 27004932 | tf_op jit(solution)/shard_map/while/body/eval_jaxpr/nhqk,nkhd->nqhd/dot_general | solution.py:76
  309.5 6.3 %fusion.50 = f32[2,512,3072]{2,1,0:T(8,128)} fusion(bf16[2,3072,1,128]{3,1,0,2:T(8,128)(2,1)S(1)} %get-tuple-element.110, bf16[6,2,512,1,128]{4,2,0,1,3:T(8,128)(2,1)S(1)} %get-tuple-element.109, s32[]{:T(128)S(6)} %copy.70), kind=kOutput, calls=%fused_computation.8.clone.1 | convolution fusion | flops 805306368 | bytes 14417924 | tf_op jit(solution)/shard_map/while/body/eval_jaxpr/nqhd,nkhd->nhqk/dot_general | solution.py:72
  315.8 11.2 %fusion.51 = f32[2,512]{1,0:T(2,128)S(1)} fusion(f32[2,512,3072]{2,1,0:T(8,128)} %fusion.50), kind=kOutput, calls=%fused_computation.37.clone.1 | output fusion | flops 12585983 | bytes 12587008 | tf_op jit(solution)/shard_map/while/body/eval_jaxpr/sub | solution.py:75
  327.0 11.4 %fusion.52 = bf16[6,2,512,1,128]{4,2,1,3,0:T(8,128)(2,1)} fusion(bf16[6,2,512,1,128]{4,2,1,3,0:T(8,128)(2,1)} %get-tuple-element.102, s32[]{:T(128)S(6)} %copy.70, bf16[2,3072,1,128]{3,1,0,2:T(8,128)(2,1)} %get-tuple-element.111, f32[2,512]{1,0:T(2,128)S(1)} %fusion.51, f32[2,512,3072]{2,1,0:T(8,128)} %fusion.50), kind=kOutput, calls=%fused_computation.12.clone.1 | convolution fusion | flops 821170176 | bytes 27004932 | tf_op jit(solution)/shard_map/while/body/eval_jaxpr/nhqk,nkhd->nqhd/dot_general | solution.py:76
  341.1 4.9 %all-to-all-start.6 = ((bf16[32,96,128]{2,1,0:T(8,128)(2,1)}), bf16[32,96,128]{2,1,0:T(8,128)(2,1)S(1)}, u32[]{:S(2)}, u32[]{:S(2)}) async-start(bf16[32,96,128]{2,1,0:T(8,128)(2,1)} %fusion.33), calls=%async_computation.6 | async-start | bytes 1572864 | tf_op jit(solution)/shard_map/all_to_all | solution.py:92
  347.4 20.1 %all-to-all-done.6 = bf16[32,96,128]{2,1,0:T(8,128)(2,1)S(1)} async-done(((bf16[32,96,128]{2,1,0:T(8,128)(2,1)}), bf16[32,96,128]{2,1,0:T(8,128)(2,1)S(1)}, u32[]{:S(2)}, u32[]{:S(2)}) %all-to-all-start.6) | async-done | bytes 786464 | tf_op jit(solution)/shard_map/all_to_all | solution.py:92
  375.9 17.0 %collective-permute-done = bf16[96,4096]{1,0:T(8,128)(2,1)S(1)} collective-permute-done((bf16[96,4096]{1,0:T(8,128)(2,1)S(1)}, bf16[96,4096]{1,0:T(8,128)(2,1)S(1)}, u32[]{:S(2)}, u32[]{:S(2)}) %collective-permute-start) | collective-permute-done | bytes 786464 | tf_op jit(solution)/shard_map/ppermute | solution.py:47
  (34 shorter events, 27.1 us)
Async XLA Ops:
  4.1 11.3 %copy-start.1 = (bf16[1,1,2,96,4096]{4,3,2,1,0:T(8,128)(2,1)S(1)}, bf16[1,1,2,96,4096]{4,3,2,1,0:T(8,128)(2,1)}, u32[]{:S(2)}) copy-start(bf16[1,1,2,96,4096]{4,3,2,1,0:T(8,128)(2,1)} %param.11) | copy-start | bytes 4718596
  4.1 53.0 %all-to-all-start.2 = ((bf16[16,2,2,96,128]{4,3,1,2,0:T(8,128)(2,1)}), bf16[16,2,2,96,128]{4,3,1,2,0:T(8,128)(2,1)S(1)}, u32[]{:S(2)}, u32[]{:S(2)}) async-start(bf16[16,2,2,96,128]{4,3,1,2,0:T(8,128)(2,1)} %copy.43), calls=%async_computation.2 | async-start | bytes 3145728 | tf_op jit(solution)/shard_map/all_to_all | solution.py:30
  62.2 44.5 %all-to-all-start.4 = ((bf16[16,2,2,96,128]{4,3,1,2,0:T(8,128)(2,1)}), bf16[16,2,2,96,128]{4,3,1,2,0:T(8,128)(2,1)S(1)}, u32[]{:S(2)}, u32[]{:S(2)}) async-start(bf16[16,2,2,96,128]{4,3,1,2,0:T(8,128)(2,1)} %copy.48), calls=%async_computation.4 | async-start | bytes 3145728 | tf_op jit(solution)/shard_map/all_to_all | solution.py:30
  106.8 42.8 %all-to-all-start = ((bf16[16,2,2,96,128]{4,3,1,2,0:T(8,128)(2,1)}), bf16[16,2,2,96,128]{4,3,1,2,0:T(8,128)(2,1)}, u32[]{:S(2)}, u32[]{:S(2)}) async-start(bf16[16,2,2,96,128]{4,3,1,2,0:T(8,128)(2,1)} %copy.39), calls=%async_computation | async-start | bytes 3145728 | tf_op jit(solution)/shard_map/all_to_all | solution.py:30
  149.6 6.4 %all-to-all-start.5 = ((bf16[16,2,2,96,128]{4,3,0,2,1:T(8,128)(2,1)}), bf16[16,2,2,96,128]{4,3,0,2,1:T(8,128)(2,1)S(1)}, u32[]{:S(2)}, u32[]{:S(2)}) async-start(bf16[16,2,2,96,128]{4,3,0,2,1:T(8,128)(2,1)} %copy.49), calls=%async_computation.5 | async-start | bytes 3145728 | tf_op jit(solution)/shard_map/all_to_all | solution.py:30
  155.9 7.4 %all-to-all-start.1 = ((bf16[16,2,2,96,128]{4,3,0,2,1:T(8,128)(2,1)}), bf16[16,2,2,96,128]{4,3,0,2,1:T(8,128)(2,1)}, u32[]{:S(2)}, u32[]{:S(2)}) async-start(bf16[16,2,2,96,128]{4,3,0,2,1:T(8,128)(2,1)} %copy.40), calls=%async_computation.1 | async-start | bytes 3145728 | tf_op jit(solution)/shard_map/all_to_all | solution.py:30
  339.9 6.8 %copy-start.2 = (bf16[1,4096]{1,0:T(2,128)(2,1)S(1)}, bf16[1,4096]{1,0:T(2,128)(2,1)}, u32[]{:S(2)}) copy-start(bf16[1,4096]{1,0:T(2,128)(2,1)} %param.13) | copy-start | bytes 24580
  341.1 26.4 %all-to-all-start.6 = ((bf16[32,96,128]{2,1,0:T(8,128)(2,1)}), bf16[32,96,128]{2,1,0:T(8,128)(2,1)S(1)}, u32[]{:S(2)}, u32[]{:S(2)}) async-start(bf16[32,96,128]{2,1,0:T(8,128)(2,1)} %fusion.33), calls=%async_computation.6 | async-start | bytes 1572864 | tf_op jit(solution)/shard_map/all_to_all | solution.py:92
  370.9 1.9 copy-start
  374.6 18.4 %collective-permute-start = (bf16[96,4096]{1,0:T(8,128)(2,1)S(1)}, bf16[96,4096]{1,0:T(8,128)(2,1)S(1)}, u32[]{:S(2)}, u32[]{:S(2)}) collective-permute-start(bf16[96,4096]{1,0:T(8,128)(2,1)S(1)} %fusion.31), channel_id=1, source_target_pairs={{0,128},{128,0},{1,129},{129,1},{2,130},{130,2},{3,131},{131,3},{4... | collective-permute-start | bytes 2359304 | tf_op jit(solution)/shard_map/ppermute | solution.py:47
where the time goes:
time: 395 us; the launch traced here: 394 us
  waiting for transfers between devices  151 us (38%)
  matrix products  106 us (27%)
  other arithmetic  73.9 us (19%)
  starting transfers between devices  33.7 us (9%)
  local copies, waits for them, and re-layouts  21.8 us (6%)
  blocking collectives  5 us (1%)
    all_to_all x5, waiting for transfers between devices, exchange_in_order(): out = lax.all_to_all(out, axes[k], k, k, tiled=True)  114 us
    dot_general x6, matrix products, one_block(): jnp.einsum('nhqk,nkhd->nqhd', weights, value_rows, preferred_element_type...  68.3 us
    sub x6, other arithmetic, one_block(): weights = jax.nn.softmax(scores, axis=-1).astype(jnp.bfloat16)  67.1 us
    dot_general x6, matrix products, one_block(): jnp.einsum('nqhd,nkhd->nhqk', query_part, key_rows, preferred_element_typ...  38 us
    all_to_all x5, starting transfers between devices, exchange_in_order(): out = lax.all_to_all(out, axes[k], k, k, tiled=True)  28.7 us
    all_to_all x1, waiting for transfers between devices, per_device(): lax.all_to_all(combine(attended[0], attended[1]), SEQ, split_axis=0, conc...  20.1 us
    ppermute x1, waiting for transfers between devices, from_partner(): return lax.ppermute(block, axis, route)  17 us
  transfers between devices with their start and end apart: 7, of which 6 were waited for; matrix products, arithmetic and copies ran while one was open for 3% of the time, Pallas kernels for 0%

commit v1 on v0

--- a/solution.py
+++ b/solution.py
@@ -89,8 +89,14 @@
             exchange_by_chip(values[0, 0], (("seq_0", "seq_1"), "seq_2"), (0, 1), 2, 1),
         )
     )
-    guided = lax.all_to_all(
-        combine(attended[0], attended[1]), SEQ, split_axis=0, concat_axis=1, tiled=True
+    guided = jnp.concatenate(
+        lax.all_to_all(
+            jnp.stack(jnp.split(combine(attended[0], attended[1]), lax.axis_size(SEQ), axis=0)),
+            SEQ,
+            0,
+            0,
+        ),
+        axis=1,
     )
     guided_f32 = guided.astype(jnp.float32)
     scale = lax.rsqrt(jnp.mean(guided_f32 * guided_f32, axis=-1, keepdims=True) + 1e-06)

time: 395 us -> 415 us (1.051)
  local copies, waits for them, and re-layouts: 21.8 us -> 38 us
  blocking collectives: 5 us -> 12.8 us
  starting transfers between devices: 33.7 us -> 28.1 us
    unnamed x9 -> x42, local copies, waits for them, and re-layouts: 3.83 us -> 24.8 us
    all_to_all x1 -> x2, blocking collectives: 5 us -> 12.8 us  [exchange_in_order(): out = lax.all_to_all(out, axes[k], k, k, tiled=True)]
    all_to_all x5 -> x4, starting transfers between devices: 28.7 us -> 22.4 us  [exchange_in_order(): out = lax.all_to_all(out, axes[k], k, k, tiled=True)]
    all_to_all x5 -> x4, waiting for transfers between devices: 114 us -> 114 us  [exchange_in_order(): out = lax.all_to_all(out, axes[k], k, k, tiled=True)]
  transfers between devices with their start and end apart: 7 -> 6, of which waited for: 6 -> 6; matrix products, arithmetic and copies ran while one was open for 3% -> 3% of each run, Pallas kernels for 0% -> 0%
where the time goes in v1:
time: 415 us; the launch traced here: 414 us
  waiting for transfers between devices  153 us (37%)
  matrix products  106 us (26%)
  other arithmetic  73.8 us (18%)
  local copies, waits for them, and re-layouts  38 us (9%)
  starting transfers between devices  28.1 us (7%)
  blocking collectives  12.8 us (3%)
    all_to_all x4, waiting for transfers between devices, exchange_in_order(): out = lax.all_to_all(out, axes[k], k, k, tiled=True)  114 us
    dot_general x6, matrix products, one_block(): jnp.einsum('nhqk,nkhd->nqhd', weights, value_rows, preferred_element_type...  68.4 us
    sub x6, other arithmetic, one_block(): weights = jax.nn.softmax(scores, axis=-1).astype(jnp.bfloat16)  67.1 us
    dot_general x6, matrix products, one_block(): jnp.einsum('nqhd,nkhd->nhqk', query_part, key_rows, preferred_element_typ...  38 us
    unnamed x42, local copies, waits for them, and re-layouts  24.8 us
    all_to_all x4, starting transfers between devices, exchange_in_order(): out = lax.all_to_all(out, axes[k], k, k, tiled=True)  22.4 us
    all_to_all x1, waiting for transfers between devices, per_device(): lax.all_to_all(jnp.stack(jnp.split(combine(attended[0], attended[1]), lax...  22.2 us
    ppermute x1, waiting for transfers between devices, from_partner(): return lax.ppermute(block, axis, route)  16.3 us
  transfers between devices with their start and end apart: 6, of which 6 were waited for; matrix products, arithmetic and copies ran while one was open for 3% of the time, Pallas kernels for 0%

profile of v1, /device:TPU:6, one launch (start us, length us, event | category | flops | bytes accessed | tf_op | source)
XLA Modules:
  0.0 414.1 jit_solution(17357988313977811335)
XLA Ops:
  4.1 11.3 %all-to-all-start.2 = ((bf16[16,2,2,96,128]{4,3,1,2,0:T(8,128)(2,1)}), bf16[16,2,2,96,128]{4,3,1,2,0:T(8,128)(2,1)S(1)}, u32[]{:S(2)}, u32[]{:S(2)}) async-start(bf16[16,2,2,96,128]{4,3,1,2,0:T(8,128)(2,1)} %copy.76), calls=%async_computation.2 | async-start | bytes 3145728 | tf_op jit(solution)/shard_map/all_to_all | solution.py:30
  17.6 39.5 %all-to-all-done.2 = bf16[16,2,2,96,128]{4,3,1,2,0:T(8,128)(2,1)S(1)} async-done(((bf16[16,2,2,96,128]{4,3,1,2,0:T(8,128)(2,1)}), bf16[16,2,2,96,128]{4,3,1,2,0:T(8,128)(2,1)S(1)}, u32[]{:S(2)}, u32[]{:S(2)}) %all-to-all-start.2) | async-done | bytes 1572896 | tf_op jit(solution)/shard_map/all_to_all | solution.py:30
  57.1 3.7 all-to-all-start.4
  65.6 35.8 %all-to-all-done.4 = bf16[16,2,2,96,128]{4,3,1,2,0:T(8,128)(2,1)S(1)} async-done(((bf16[16,2,2,96,128]{4,3,1,2,0:T(8,128)(2,1)}), bf16[16,2,2,96,128]{4,3,1,2,0:T(8,128)(2,1)S(1)}, u32[]{:S(2)}, u32[]{:S(2)}) %all-to-all-start.4) | async-done | bytes 1572896 | tf_op jit(solution)/shard_map/all_to_all | solution.py:30
  101.5 3.7 all-to-all-start.3
  107.6 7.8 %all_to_all.35 = bf16[16,2,2,96,128]{4,3,0,2,1:T(8,128)(2,1)} all-to-all(bf16[16,2,2,96,128]{4,3,0,2,1:T(8,128)(2,1)} %copy.82), channel_id=1, replica_groups=mesh['expert'=2,'batch'=4,'seq_0'=4,'seq_1'=4,'seq_2'=2] {'seq_2'}, dimensions={1} | all-to-all | bytes 3145728 | tf_op jit(solution)/shard_map/all_to_all | solution.py:30
  115.5 3.7 all-to-all-start
  122.3 37.7 %all-to-all-done = bf16[16,2,2,96,128]{4,3,1,2,0:T(8,128)(2,1)S(1)} async-done(((bf16[16,2,2,96,128]{4,3,1,2,0:T(8,128)(2,1)}), bf16[16,2,2,96,128]{4,3,1,2,0:T(8,128)(2,1)S(1)}, u32[]{:S(2)}, u32[]{:S(2)}) %all-to-all-start) | async-done | bytes 1572896 | tf_op jit(solution)/shard_map/all_to_all | solution.py:30
  160.1 5.0 %all_to_all.36 = bf16[16,2,2,96,128]{4,3,0,2,1:T(8,128)(2,1)S(1)} all-to-all(bf16[16,2,2,96,128]{4,3,0,2,1:T(8,128)(2,1)S(1)} %copy.73), channel_id=1, replica_groups=mesh['expert'=2,'batch'=4,'seq_0'=4,'seq_1'=4,'seq_2'=2] {'seq_2'}, dimensions={1} | all-to-all | bytes 3145728 | tf_op jit(solution)/shard_map/all_to_all | solution.py:30
  165.2 173.5 %while.10 = (s32[]{:T(128)}, bf16[6,2,512,1,128]{4,2,1,3,0:T(8,128)(2,1)}, bf16[6,2,512,1,128]{4,2,0,1,3:T(8,128)(2,1)S(1)}, bf16[2,3072,1,128]{3,1,0,2:T(8,128)...) while((s32[]{:T(128)}, bf16[6,2,512,1,128]{4,2,1,3,0:T(8,128)(2,1)}, ...), condition=%wide.region_3.4_spmd, body=%wide.region_0.3_spmd.sunk | while | flops 1639062528 | bytes 54010440 | solution.py:80
  165.2 6.3 %fusion.50 = f32[2,512,3072]{2,1,0:T(8,128)} fusion(bf16[2,3072,1,128]{3,1,0,2:T(8,128)(2,1)S(1)} %get-tuple-element.115, bf16[6,2,512,1,128]{4,2,0,1,3:T(8,128)(2,1)S(1)} %get-tuple-element.114, s32[]{:T(128)} %get-tuple-element.106), kind=kOutput, calls=%fused_computation.8.clone.1 | convolution fusion | flops 805306368 | bytes 14417924 | tf_op jit(solution)/shard_map/while/body/eval_jaxpr/nqhd,nkhd->nhqk/dot_general | solution.py:72
  171.6 11.2 %fusion.51 = f32[2,512]{1,0:T(2,128)S(1)} fusion(f32[2,512,3072]{2,1,0:T(8,128)} %fusion.50), kind=kOutput, calls=%fused_computation.101.clone.1 | output fusion | flops 12585983 | bytes 12587008 | tf_op jit(solution)/shard_map/while/body/eval_jaxpr/sub | solution.py:75
  182.8 11.4 %fusion.52 = bf16[6,2,512,1,128]{4,2,1,3,0:T(8,128)(2,1)} fusion(bf16[6,2,512,1,128]{4,2,1,3,0:T(8,128)(2,1)} %get-tuple-element.107, s32[]{:T(128)} %get-tuple-element.106, bf16[2,3072,1,128]{3,1,0,2:T(8,128)(2,1)} %get-tuple-element.116, f32[2,512]{1,0:T(2,128)S(1)} %fusion.51, f32[2,512,3072]{2,1,0:T(8,128)} %fusion.50), kind=kOutput, calls=%fused_computation.12.clone.1 | convolution fusion | flops 821170176 | bytes 27005440 | tf_op jit(solution)/shard_map/while/body/eval_jaxpr/nhqk,nkhd->nqhd/dot_general | solution.py:76
  194.2 6.3 %fusion.50 = f32[2,512,3072]{2,1,0:T(8,128)} fusion(bf16[2,3072,1,128]{3,1,0,2:T(8,128)(2,1)S(1)} %get-tuple-element.115, bf16[6,2,512,1,128]{4,2,0,1,3:T(8,128)(2,1)S(1)} %get-tuple-element.114, s32[]{:T(128)} %get-tuple-element.106), kind=kOutput, calls=%fused_computation.8.clone.1 | convolution fusion | flops 805306368 | bytes 14417924 | tf_op jit(solution)/shard_map/while/body/eval_jaxpr/nqhd,nkhd->nhqk/dot_general | solution.py:72
  200.5 11.2 %fusion.51 = f32[2,512]{1,0:T(2,128)S(1)} fusion(f32[2,512,3072]{2,1,0:T(8,128)} %fusion.50), kind=kOutput, calls=%fused_computation.101.clone.1 | output fusion | flops 12585983 | bytes 12587008 | tf_op jit(solution)/shard_map/while/body/eval_jaxpr/sub | solution.py:75
  211.7 11.4 %fusion.52 = bf16[6,2,512,1,128]{4,2,1,3,0:T(8,128)(2,1)} fusion(bf16[6,2,512,1,128]{4,2,1,3,0:T(8,128)(2,1)} %get-tuple-element.107, s32[]{:T(128)} %get-tuple-element.106, bf16[2,3072,1,128]{3,1,0,2:T(8,128)(2,1)} %get-tuple-element.116, f32[2,512]{1,0:T(2,128)S(1)} %fusion.51, f32[2,512,3072]{2,1,0:T(8,128)} %fusion.50), kind=kOutput, calls=%fused_computation.12.clone.1 | convolution fusion | flops 821170176 | bytes 27005440 | tf_op jit(solution)/shard_map/while/body/eval_jaxpr/nhqk,nkhd->nqhd/dot_general | solution.py:76
  223.1 6.3 %fusion.50 = f32[2,512,3072]{2,1,0:T(8,128)} fusion(bf16[2,3072,1,128]{3,1,0,2:T(8,128)(2,1)S(1)} %get-tuple-element.115, bf16[6,2,512,1,128]{4,2,0,1,3:T(8,128)(2,1)S(1)} %get-tuple-element.114, s32[]{:T(128)} %get-tuple-element.106), kind=kOutput, calls=%fused_computation.8.clone.1 | convolution fusion | flops 805306368 | bytes 14417924 | tf_op jit(solution)/shard_map/while/body/eval_jaxpr/nqhd,nkhd->nhqk/dot_general | solution.py:72
  229.4 11.2 %fusion.51 = f32[2,512]{1,0:T(2,128)S(1)} fusion(f32[2,512,3072]{2,1,0:T(8,128)} %fusion.50), kind=kOutput, calls=%fused_computation.101.clone.1 | output fusion | flops 12585983 | bytes 12587008 | tf_op jit(solution)/shard_map/while/body/eval_jaxpr/sub | solution.py:75
  240.6 11.4 %fusion.52 = bf16[6,2,512,1,128]{4,2,1,3,0:T(8,128)(2,1)} fusion(bf16[6,2,512,1,128]{4,2,1,3,0:T(8,128)(2,1)} %get-tuple-element.107, s32[]{:T(128)} %get-tuple-element.106, bf16[2,3072,1,128]{3,1,0,2:T(8,128)(2,1)} %get-tuple-element.116, f32[2,512]{1,0:T(2,128)S(1)} %fusion.51, f32[2,512,3072]{2,1,0:T(8,128)} %fusion.50), kind=kOutput, calls=%fused_computation.12.clone.1 | convolution fusion | flops 821170176 | bytes 27005440 | tf_op jit(solution)/shard_map/while/body/eval_jaxpr/nhqk,nkhd->nqhd/dot_general | solution.py:76
  252.0 6.3 %fusion.50 = f32[2,512,3072]{2,1,0:T(8,128)} fusion(bf16[2,3072,1,128]{3,1,0,2:T(8,128)(2,1)S(1)} %get-tuple-element.115, bf16[6,2,512,1,128]{4,2,0,1,3:T(8,128)(2,1)S(1)} %get-tuple-element.114, s32[]{:T(128)} %get-tuple-element.106), kind=kOutput, calls=%fused_computation.8.clone.1 | convolution fusion | flops 805306368 | bytes 14417924 | tf_op jit(solution)/shard_map/while/body/eval_jaxpr/nqhd,nkhd->nhqk/dot_general | solution.py:72
  258.3 11.2 %fusion.51 = f32[2,512]{1,0:T(2,128)S(1)} fusion(f32[2,512,3072]{2,1,0:T(8,128)} %fusion.50), kind=kOutput, calls=%fused_computation.101.clone.1 | output fusion | flops 12585983 | bytes 12587008 | tf_op jit(solution)/shard_map/while/body/eval_jaxpr/sub | solution.py:75
  269.5 11.4 %fusion.52 = bf16[6,2,512,1,128]{4,2,1,3,0:T(8,128)(2,1)} fusion(bf16[6,2,512,1,128]{4,2,1,3,0:T(8,128)(2,1)} %get-tuple-element.107, s32[]{:T(128)} %get-tuple-element.106, bf16[2,3072,1,128]{3,1,0,2:T(8,128)(2,1)} %get-tuple-element.116, f32[2,512]{1,0:T(2,128)S(1)} %fusion.51, f32[2,512,3072]{2,1,0:T(8,128)} %fusion.50), kind=kOutput, calls=%fused_computation.12.clone.1 | convolution fusion | flops 821170176 | bytes 27005440 | tf_op jit(solution)/shard_map/while/body/eval_jaxpr/nhqk,nkhd->nqhd/dot_general | solution.py:76
  280.9 6.3 %fusion.50 = f32[2,512,3072]{2,1,0:T(8,128)} fusion(bf16[2,3072,1,128]{3,1,0,2:T(8,128)(2,1)S(1)} %get-tuple-element.115, bf16[6,2,512,1,128]{4,2,0,1,3:T(8,128)(2,1)S(1)} %get-tuple-element.114, s32[]{:T(128)} %get-tuple-element.106), kind=kOutput, calls=%fused_computation.8.clone.1 | convolution fusion | flops 805306368 | bytes 14417924 | tf_op jit(solution)/shard_map/while/body/eval_jaxpr/nqhd,nkhd->nhqk/dot_general | solution.py:72
  287.3 11.2 %fusion.51 = f32[2,512]{1,0:T(2,128)S(1)} fusion(f32[2,512,3072]{2,1,0:T(8,128)} %fusion.50), kind=kOutput, calls=%fused_computation.101.clone.1 | output fusion | flops 12585983 | bytes 12587008 | tf_op jit(solution)/shard_map/while/body/eval_jaxpr/sub | solution.py:75
  298.4 11.4 %fusion.52 = bf16[6,2,512,1,128]{4,2,1,3,0:T(8,128)(2,1)} fusion(bf16[6,2,512,1,128]{4,2,1,3,0:T(8,128)(2,1)} %get-tuple-element.107, s32[]{:T(128)} %get-tuple-element.106, bf16[2,3072,1,128]{3,1,0,2:T(8,128)(2,1)} %get-tuple-element.116, f32[2,512]{1,0:T(2,128)S(1)} %fusion.51, f32[2,512,3072]{2,1,0:T(8,128)} %fusion.50), kind=kOutput, calls=%fused_computation.12.clone.1 | convolution fusion | flops 821170176 | bytes 27005440 | tf_op jit(solution)/shard_map/while/body/eval_jaxpr/nhqk,nkhd->nqhd/dot_general | solution.py:76
  309.8 6.3 %fusion.50 = f32[2,512,3072]{2,1,0:T(8,128)} fusion(bf16[2,3072,1,128]{3,1,0,2:T(8,128)(2,1)S(1)} %get-tuple-element.115, bf16[6,2,512,1,128]{4,2,0,1,3:T(8,128)(2,1)S(1)} %get-tuple-element.114, s32[]{:T(128)} %get-tuple-element.106), kind=kOutput, calls=%fused_computation.8.clone.1 | convolution fusion | flops 805306368 | bytes 14417924 | tf_op jit(solution)/shard_map/while/body/eval_jaxpr/nqhd,nkhd->nhqk/dot_general | solution.py:72
  316.2 11.2 %fusion.51 = f32[2,512]{1,0:T(2,128)S(1)} fusion(f32[2,512,3072]{2,1,0:T(8,128)} %fusion.50), kind=kOutput, calls=%fused_computation.101.clone.1 | output fusion | flops 12585983 | bytes 12587008 | tf_op jit(solution)/shard_map/while/body/eval_jaxpr/sub | solution.py:75
  327.4 11.4 %fusion.52 = bf16[6,2,512,1,128]{4,2,1,3,0:T(8,128)(2,1)} fusion(bf16[6,2,512,1,128]{4,2,1,3,0:T(8,128)(2,1)} %get-tuple-element.107, s32[]{:T(128)} %get-tuple-element.106, bf16[2,3072,1,128]{3,1,0,2:T(8,128)(2,1)} %get-tuple-element.116, f32[2,512]{1,0:T(2,128)S(1)} %fusion.51, f32[2,512,3072]{2,1,0:T(8,128)} %fusion.50), kind=kOutput, calls=%fused_computation.12.clone.1 | convolution fusion | flops 821170176 | bytes 27005440 | tf_op jit(solution)/shard_map/while/body/eval_jaxpr/nhqk,nkhd->nqhd/dot_general | solution.py:76
  360.2 5.7 %all-to-all-start.6 = ((bf16[32,96,128]{2,1,0:T(8,128)(2,1)}), bf16[32,96,128]{2,1,0:T(8,128)(2,1)S(1)}, u32[]{:S(2)}, u32[]{:S(2)}) async-start(bf16[32,96,128]{2,1,0:T(8,128)(2,1)} %constant_dynamic-update-slice_fusion), calls=%async_computation.6 | async-start | bytes 1572864 | tf_op jit(solution)/shard_map/all_to_all | solution.py:93
  367.3 22.2 %all-to-all-done.6 = bf16[32,96,128]{2,1,0:T(8,128)(2,1)S(1)} async-done(((bf16[32,96,128]{2,1,0:T(8,128)(2,1)}), bf16[32,96,128]{2,1,0:T(8,128)(2,1)S(1)}, u32[]{:S(2)}, u32[]{:S(2)}) %all-to-all-start.6) | async-done | bytes 786464 | tf_op jit(solution)/shard_map/all_to_all | solution.py:93
  393.3 2.4 fusion.29
  395.7 16.3 %collective-permute-done = bf16[96,4096]{1,0:T(8,128)(2,1)} collective-permute-done((bf16[96,4096]{1,0:T(8,128)(2,1)}, bf16[96,4096]{1,0:T(8,128)(2,1)}, u32[]{:S(2)}, u32[]{:S(2)}) %collective-permute-start) | collective-permute-done | bytes 786464 | tf_op jit(solution)/shard_map/ppermute | solution.py:47
  (67 shorter events, 43.6 us)
Async XLA Ops:
  4.1 11.3 %copy-start.2 = (bf16[1,1,2,96,4096]{4,3,2,1,0:T(8,128)(2,1)S(1)}, bf16[1,1,2,96,4096]{4,3,2,1,0:T(8,128)(2,1)}, u32[]{:S(2)}) copy-start(bf16[1,1,2,96,4096]{4,3,2,1,0:T(8,128)(2,1)} %param.11) | copy-start | bytes 4718596
  4.1 53.0 %all-to-all-start.2 = ((bf16[16,2,2,96,128]{4,3,1,2,0:T(8,128)(2,1)}), bf16[16,2,2,96,128]{4,3,1,2,0:T(8,128)(2,1)S(1)}, u32[]{:S(2)}, u32[]{:S(2)}) async-start(bf16[16,2,2,96,128]{4,3,1,2,0:T(8,128)(2,1)} %copy.76), calls=%async_computation.2 | async-start | bytes 3145728 | tf_op jit(solution)/shard_map/all_to_all | solution.py:30
  57.1 44.4 %all-to-all-start.4 = ((bf16[16,2,2,96,128]{4,3,1,2,0:T(8,128)(2,1)}), bf16[16,2,2,96,128]{4,3,1,2,0:T(8,128)(2,1)S(1)}, u32[]{:S(2)}, u32[]{:S(2)}) async-start(bf16[16,2,2,96,128]{4,3,1,2,0:T(8,128)(2,1)} %copy.81), calls=%async_computation.4 | async-start | bytes 3145728 | tf_op jit(solution)/shard_map/all_to_all | solution.py:30
  101.5 6.2 %all-to-all-start.3 = ((bf16[16,2,2,96,128]{4,3,0,2,1:T(8,128)(2,1)}), bf16[16,2,2,96,128]{4,3,0,2,1:T(8,128)(2,1)S(1)}, u32[]{:S(2)}, u32[]{:S(2)}) async-start(bf16[16,2,2,96,128]{4,3,0,2,1:T(8,128)(2,1)} %copy.77), calls=%async_computation.3 | async-start | bytes 3145728 | tf_op jit(solution)/shard_map/all_to_all | solution.py:30
  115.5 44.5 %all-to-all-start = ((bf16[16,2,2,96,128]{4,3,1,2,0:T(8,128)(2,1)}), bf16[16,2,2,96,128]{4,3,1,2,0:T(8,128)(2,1)S(1)}, u32[]{:S(2)}, u32[]{:S(2)}) async-start(bf16[16,2,2,96,128]{4,3,1,2,0:T(8,128)(2,1)} %copy.72), calls=%async_computation | async-start | bytes 3145728 | tf_op jit(solution)/shard_map/all_to_all | solution.py:30
  119.4 1.4 copy-start
  341.3 25.2 %copy-start.3 = (bf16[1,4096]{1,0:T(2,128)(2,1)S(1)}, bf16[1,4096]{1,0:T(2,128)(2,1)}, u32[]{:S(2)}) copy-start(bf16[1,4096]{1,0:T(2,128)(2,1)} %param.13) | copy-start | bytes 24580
  360.2 29.3 %all-to-all-start.6 = ((bf16[32,96,128]{2,1,0:T(8,128)(2,1)}), bf16[32,96,128]{2,1,0:T(8,128)(2,1)S(1)}, u32[]{:S(2)}, u32[]{:S(2)}) async-start(bf16[32,96,128]{2,1,0:T(8,128)(2,1)} %constant_dynamic-update-slice_fusion), calls=%async_computation.6 | async-start | bytes 1572864 | tf_op jit(solution)/shard_map/all_to_all | solution.py:93
  389.7 1.1 copy-start.1
  392.1 19.9 %collective-permute-start = (bf16[96,4096]{1,0:T(8,128)(2,1)}, bf16[96,4096]{1,0:T(8,128)(2,1)}, u32[]{:S(2)}, u32[]{:S(2)}) collective-permute-start(bf16[96,4096]{1,0:T(8,128)(2,1)} %fusion.31), channel_id=1, source_target_pairs={{0,128},{128,0},{1,129},{129,1},{2,130},{130,2},{3,131},{131,3},{4... | collective-permute-start | bytes 2359304 | tf_op jit(solution)/shard_map/ppermute | solution.py:47
